TPU v7x, 32 devices: a whole 2x2x4 slice. The times are simulated.
32 devices in a mesh: grp: 2 (over core), ctx: 4 (over z), wsh: 4 (over y, x).
Axes of the slice: x: 2, y: 2, z: 4, core: 2. Of those that a mesh axis runs over, the one named last changes fastest.
Arguments:
- tokens: bfloat16 [6144, 1152], P(('grp', 'ctx', 'wsh')), may hold values from -6 to 6
- segment_ids: int32 [6144], P(('grp', 'ctx', 'wsh')), may hold values from 0 to 1, as said below
- positions: int32 [6144], P(('grp', 'ctx', 'wsh')), may hold values from 0 to 3071, as said below
- attend_gain: float32 [1152], replicated, may hold values from 0.5 to 1.5
- query_key_value: bfloat16 [1152, 1920], P('wsh'), may hold values from -0.25 to 0.25
- attend_out: bfloat16 [1152, 1152], P('wsh'), may hold values from -2 to 2
- feed_gain: float32 [1152], replicated, may hold values from 0.5 to 1.5
- gate_up: bfloat16 [1152, 6144], P('wsh'), may hold values from -0.1875 to 0.1875
- down_weight: bfloat16 [3072, 1152], P('wsh'), may hold values from -0.4375 to 0.4375
- upstream: bfloat16 [6144, 1152], P(('grp', 'ctx', 'wsh')), may hold values from -6 to 6
Outputs:
- activations: bfloat16 [6144, 1152], P(('grp', 'ctx', 'wsh'))
- input_grad: float32 [6144, 1152], P(('grp', 'ctx', 'wsh'))
- query_key_value_grad: float32 [1152, 1920], P(('ctx', 'wsh'))
- attend_out_grad: float32 [1152, 1152], P(('ctx', 'wsh'))
- gate_up_grad: float32 [1152, 6144], P(('ctx', 'wsh'))
- down_weight_grad: float32 [3072, 1152], P(('ctx', 'wsh'))
- attend_gain_grad: float32 [1152], P(('ctx', 'wsh'))
- feed_gain_grad: float32 [1152], P(('ctx', 'wsh'))
Inputs may be any that keep to these rules, and one draw needn't show every extreme that they name: `segment_ids`: in each group of 3072 rows the aligned runs of 96 rows are the runs of 96 consecutive tokens of that group's token stream, in some order, each once; the stream is the prompt of 2048 tokens (segment 0) followed by 1 continuations of 1024 tokens (segments 1 to 1). `positions`: matching segment_ids: a prompt token's position is its index in the prompt; a continuation token's position is 2048 plus its index in its continuation.
All inputs are finite; a program needn't handle non-finite values.
Results may differ from a plain program's by a relative error of at most 0.02.
Values may be sent and summed in bfloat16 or wider, within the bound.
A program may use at most 256 MiB of HBM per device.

v0:
```python
import math
import jax
import jax.numpy as jnp
from jax import lax
from jax.sharding import PartitionSpec as P

HEADS = 18
KV_HEADS = 6
HEAD_DIM = 64
FF = 3072
KTILE = 1024
QW = 1152
KW = 384
EPSILON = 1e-05


def rope_angles(positions):
    halfway = HEAD_DIM // 2
    frequency = jnp.exp(jnp.arange(halfway, dtype=jnp.float32) * (-math.log(10000.0) / halfway))
    angles = positions.astype(jnp.float32)[:, None] * frequency[None, :]
    return (jnp.cos(angles), jnp.sin(angles))


def rotate(tensor, cosine, sine_table):
    halfway = tensor.shape[-1] // 2
    first_half = tensor[..., :halfway]
    second_half = tensor[..., halfway:]
    cos_wide = cosine[:, None, :]
    sin_wide = sine_table[:, None, :]
    return jnp.concatenate(
        [
            first_half * cos_wide - second_half * sin_wide,
            second_half * cos_wide + first_half * sin_wide,
        ],
        axis=-1,
    )


def unrotate(gradient, cosine, sine_table):
    halfway = gradient.shape[-1] // 2
    first_half = gradient[..., :halfway]
    second_half = gradient[..., halfway:]
    cos_wide = cosine[:, None, :]
    sin_wide = sine_table[:, None, :]
    return jnp.concatenate(
        [
            first_half * cos_wide + second_half * sin_wide,
            second_half * cos_wide - first_half * sin_wide,
        ],
        axis=-1,
    )


def rms_factor(values):
    return lax.rsqrt(jnp.mean(values * values, axis=-1, keepdims=True) + EPSILON)


def norm_back(grad_normed, inputs, factor, gain):
    weighted = grad_normed * gain
    inner_mean = jnp.mean(weighted * inputs, axis=-1, keepdims=True)
    input_part = factor * weighted - inputs * (factor * factor * factor) * inner_mean
    return (input_part, jnp.sum(grad_normed * inputs * factor, axis=0))


def rounded(values):
    return lax.optimization_barrier(values.astype(jnp.bfloat16)).astype(jnp.float32)


def tile_mask(segment_ids, positions, seg_key, pos_key):
    return (pos_key[None, :] <= positions[:, None]) & (
        (seg_key[None, :] == 0) | (seg_key[None, :] == segment_ids[:, None])
    )


def tile_scores(queries, key_tile, allowed):
    raw_scores = jnp.einsum(
        "nhjd,khd->hjnk", queries, key_tile, preferred_element_type=jnp.float32
    ) * HEAD_DIM ** (-0.5)
    return jnp.where(allowed, raw_scores, -1e30)


def split_tiles(key_all, value_all, seg_all, pos_all):
    tile_count = key_all.shape[0] // KTILE
    key_tiles = key_all.reshape(tile_count, KTILE, KV_HEADS, HEAD_DIM)
    value_tiles = value_all.reshape(tile_count, KTILE, KV_HEADS, HEAD_DIM)
    return (
        key_tiles,
        value_tiles,
        seg_all.reshape(tile_count, KTILE),
        pos_all.reshape(tile_count, KTILE),
    )


def attend_forward(queries, key_all, value_all, seg_all, pos_all, segment_ids, positions):
    local_rows = queries.shape[0]
    head_ratio = HEADS // KV_HEADS
    key_tiles, value_tiles, seg_tiles, pos_tiles = split_tiles(key_all, value_all, seg_all, pos_all)

    def stats_step(state_pair, pieces):
        running_max, running_sum = state_pair
        key_tile, seg_key, pos_key = pieces
        allowed = tile_mask(segment_ids, positions, seg_key, pos_key)
        scores = tile_scores(queries, key_tile, allowed)
        new_max = jnp.maximum(running_max, jnp.max(scores, axis=-1))
        expons = jnp.where(allowed, jnp.exp(scores - new_max[..., None]), 0.0)
        new_sum = running_sum * jnp.exp(running_max - new_max) + jnp.sum(expons, axis=-1)
        return ((new_max, new_sum), None)

    start_max = jnp.full((KV_HEADS, head_ratio, local_rows), -1e30, jnp.float32)
    start_sum = jnp.zeros((KV_HEADS, head_ratio, local_rows), jnp.float32)
    (row_max, row_sum), _ = lax.scan(
        stats_step, (start_max, start_sum), (key_tiles, seg_tiles, pos_tiles)
    )
    log_total = row_max + jnp.log(row_sum)

    def value_step(running, pieces):
        key_tile, value_tile, seg_key, pos_key = pieces
        allowed = tile_mask(segment_ids, positions, seg_key, pos_key)
        scores = tile_scores(queries, key_tile, allowed)
        weights_tile = jnp.where(allowed, jnp.exp(scores - log_total[..., None]), 0.0).astype(
            jnp.bfloat16
        )
        return (
            running
            + jnp.einsum(
                "hjnk,khd->nhjd", weights_tile, value_tile, preferred_element_type=jnp.float32
            ),
            None,
        )

    start_out = jnp.zeros((local_rows, KV_HEADS, head_ratio, HEAD_DIM), jnp.float32)
    output, _ = lax.scan(value_step, start_out, (key_tiles, value_tiles, seg_tiles, pos_tiles))
    return (output, log_total)


def attend_backward(
    queries,
    key_all,
    value_all,
    seg_all,
    pos_all,
    segment_ids,
    positions,
    log_total,
    output_grad,
    output,
):
    key_count = key_all.shape[0]
    key_tiles, value_tiles, seg_tiles, pos_tiles = split_tiles(key_all, value_all, seg_all, pos_all)
    row_delta = jnp.einsum("nhjd,nhjd->hjn", output_grad.astype(jnp.float32), output)

    def grad_step(query_sum, pieces):
        key_tile, value_tile, seg_key, pos_key = pieces
        allowed = tile_mask(segment_ids, positions, seg_key, pos_key)
        scores = tile_scores(queries, key_tile, allowed)
        weights_tile = jnp.where(allowed, jnp.exp(scores - log_total[..., None]), 0.0)
        value_grad = jnp.einsum(
            "hjnk,nhjd->khd",
            weights_tile.astype(jnp.bfloat16),
            output_grad,
            preferred_element_type=jnp.float32,
        )
        weight_grad = jnp.einsum(
            "nhjd,khd->hjnk", output_grad, value_tile, preferred_element_type=jnp.float32
        )
        score_grad = (weights_tile * (weight_grad - row_delta[..., None])).astype(jnp.bfloat16)
        query_sum = query_sum + jnp.einsum(
            "hjnk,khd->nhjd", score_grad, key_tile, preferred_element_type=jnp.float32
        )
        key_grad = jnp.einsum(
            "hjnk,nhjd->khd", score_grad, queries, preferred_element_type=jnp.float32
        )
        return (query_sum, (key_grad, value_grad))

    start_query = jnp.zeros(queries.shape, jnp.float32)
    query_sum, (key_grads, value_grads) = lax.scan(
        grad_step, start_query, (key_tiles, value_tiles, seg_tiles, pos_tiles)
    )
    scale_factor = HEAD_DIM ** (-0.5)
    return (
        query_sum * scale_factor,
        key_grads.reshape(key_count, KW) * scale_factor,
        value_grads.reshape(key_count, KW),
    )


def local(
    tokens,
    segment_ids,
    positions,
    attend_gain,
    query_key_value,
    attend_out,
    feed_gain,
    gate_up,
    down_weight,
    upstream,
):
    local_rows = tokens.shape[0]
    head_ratio = HEADS // KV_HEADS
    inputs = tokens.astype(jnp.float32)
    factor_one = rms_factor(inputs)
    normed_one = (inputs * factor_one * attend_gain).astype(jnp.bfloat16)
    full_qkv, full_out, full_gate_up, full_down = (
        lax.all_gather(query_key_value, "wsh", axis=0, tiled=True),
        lax.all_gather(attend_out, "wsh", axis=0, tiled=True),
        lax.all_gather(gate_up, "wsh", axis=0, tiled=True),
        lax.all_gather(down_weight, "wsh", axis=0, tiled=True),
    )
    projected = jnp.dot(normed_one, full_qkv, preferred_element_type=jnp.float32)
    cosine, sine_table = rope_angles(positions)
    queries = rotate(
        projected[:, :QW].reshape(local_rows, HEADS, HEAD_DIM), cosine, sine_table
    ).astype(jnp.bfloat16)
    queries = queries.reshape(local_rows, KV_HEADS, head_ratio, HEAD_DIM)
    key_local = (
        rotate(
            projected[:, QW : QW + KW].reshape(local_rows, KV_HEADS, HEAD_DIM), cosine, sine_table
        )
        .astype(jnp.bfloat16)
        .reshape(local_rows, KW)
    )
    value_local = projected[:, QW + KW :].astype(jnp.bfloat16)
    key_all, value_all, seg_all, pos_all = (
        lax.all_gather(key_local, ("ctx", "wsh"), axis=0, tiled=True),
        lax.all_gather(value_local, ("ctx", "wsh"), axis=0, tiled=True),
        lax.all_gather(segment_ids, ("ctx", "wsh"), axis=0, tiled=True),
        lax.all_gather(positions, ("ctx", "wsh"), axis=0, tiled=True),
    )
    output, log_total = attend_forward(
        queries, key_all, value_all, seg_all, pos_all, segment_ids, positions
    )
    attended = output.reshape(local_rows, QW).astype(jnp.bfloat16)
    middle = inputs + jnp.dot(attended, full_out, preferred_element_type=jnp.float32)
    factor_two = rms_factor(middle)
    normed_two = (middle * factor_two * feed_gain).astype(jnp.bfloat16)
    gate_value = jnp.dot(normed_two, full_gate_up, preferred_element_type=jnp.float32)
    gate_part = gate_value[:, :FF]
    up_part = gate_value[:, FF:]
    sigmoid_gate = jax.nn.sigmoid(gate_part)
    silu_gate = gate_part * sigmoid_gate
    hidden = (silu_gate * up_part).astype(jnp.bfloat16)
    activations = (middle + jnp.dot(hidden, full_down, preferred_element_type=jnp.float32)).astype(
        jnp.bfloat16
    )
    back_qkv, back_out, back_gate_up, back_down = (
        lax.all_gather(query_key_value, "wsh", axis=0, tiled=True),
        lax.all_gather(attend_out, "wsh", axis=0, tiled=True),
        lax.all_gather(gate_up, "wsh", axis=0, tiled=True),
        lax.all_gather(down_weight, "wsh", axis=0, tiled=True),
    )
    down_grad = jnp.dot(hidden.T, upstream, preferred_element_type=jnp.float32)
    hidden_grad = jnp.dot(upstream, back_down.T, preferred_element_type=jnp.float32)
    gate_grad = hidden_grad * up_part * sigmoid_gate * (1.0 + gate_part * (1.0 - sigmoid_gate))
    up_grad = hidden_grad * silu_gate
    joint_grad = jnp.concatenate([gate_grad, up_grad], axis=1).astype(jnp.bfloat16)
    gate_up_grad = jnp.dot(normed_two.T, joint_grad, preferred_element_type=jnp.float32)
    normed_two_grad = jnp.dot(joint_grad, back_gate_up.T, preferred_element_type=jnp.float32)
    middle_part, feed_gain_grad = norm_back(normed_two_grad, middle, factor_two, feed_gain)
    middle_grad = upstream.astype(jnp.float32) + middle_part
    branch_grad = middle_grad.astype(jnp.bfloat16)
    out_weight_grad = jnp.dot(attended.T, branch_grad, preferred_element_type=jnp.float32)
    attended_grad = jnp.dot(branch_grad, back_out.T, preferred_element_type=jnp.float32).astype(
        jnp.bfloat16
    )
    attended_grad = attended_grad.reshape(local_rows, KV_HEADS, head_ratio, HEAD_DIM)
    query_grad, key_grad_all, value_grad_all = attend_backward(
        queries,
        key_all,
        value_all,
        seg_all,
        pos_all,
        segment_ids,
        positions,
        log_total,
        attended_grad,
        output,
    )
    key_grad, value_grad = (
        lax.psum_scatter(key_grad_all, ("ctx", "wsh"), scatter_dimension=0, tiled=True),
        lax.psum_scatter(value_grad_all, ("ctx", "wsh"), scatter_dimension=0, tiled=True),
    )
    query_back = unrotate(
        rounded(query_grad).reshape(local_rows, HEADS, HEAD_DIM), cosine, sine_table
    ).reshape(local_rows, QW)
    key_back = unrotate(
        rounded(key_grad).reshape(local_rows, KV_HEADS, HEAD_DIM), cosine, sine_table
    ).reshape(local_rows, KW)
    projected_grad = jnp.concatenate(
        [
            query_back.astype(jnp.bfloat16),
            key_back.astype(jnp.bfloat16),
            value_grad.astype(jnp.bfloat16),
        ],
        axis=1,
    )
    qkv_grad = jnp.dot(normed_one.T, projected_grad, preferred_element_type=jnp.float32)
    normed_one_grad = jnp.dot(projected_grad, back_qkv.T, preferred_element_type=jnp.float32)
    input_part, attend_gain_grad = norm_back(normed_one_grad, inputs, factor_one, attend_gain)
    input_grad = middle_grad + input_part
    shares = (
        lax.psum_scatter(qkv_grad, ("ctx", "wsh"), scatter_dimension=0, tiled=True),
        lax.psum_scatter(out_weight_grad, ("ctx", "wsh"), scatter_dimension=0, tiled=True),
        lax.psum_scatter(gate_up_grad, ("ctx", "wsh"), scatter_dimension=0, tiled=True),
        lax.psum_scatter(down_grad, ("ctx", "wsh"), scatter_dimension=0, tiled=True),
        lax.psum_scatter(attend_gain_grad, ("ctx", "wsh"), scatter_dimension=0, tiled=True),
        lax.psum_scatter(feed_gain_grad, ("ctx", "wsh"), scatter_dimension=0, tiled=True),
    )
    shares = (
        lax.psum(shares[0].astype(jnp.bfloat16), "grp").astype(jnp.float32),
        lax.psum(shares[1].astype(jnp.bfloat16), "grp").astype(jnp.float32),
        lax.psum(shares[2].astype(jnp.bfloat16), "grp").astype(jnp.float32),
        lax.psum(shares[3].astype(jnp.bfloat16), "grp").astype(jnp.float32),
        lax.psum(shares[4].astype(jnp.bfloat16), "grp").astype(jnp.float32),
        lax.psum(shares[5].astype(jnp.bfloat16), "grp").astype(jnp.float32),
    )
    return (
        activations,
        input_grad,
        shares[0],
        shares[1],
        shares[2],
        shares[3],
        shares[4],
        shares[5],
    )


def solution(mesh):
    in_specs = (
        P(("grp", "ctx", "wsh"), None),
        P(("grp", "ctx", "wsh")),
        P(("grp", "ctx", "wsh")),
        P(),
        P("wsh", None),
        P("wsh", None),
        P(),
        P("wsh", None),
        P("wsh", None),
        P(("grp", "ctx", "wsh"), None),
    )
    out_specs = (
        P(("grp", "ctx", "wsh"), None),
        P(("grp", "ctx", "wsh"), None),
        P(("ctx", "wsh"), None),
        P(("ctx", "wsh"), None),
        P(("ctx", "wsh"), None),
        P(("ctx", "wsh"), None),
        P(("ctx", "wsh")),
        P(("ctx", "wsh")),
    )
    return jax.shard_map(local, mesh=mesh, in_specs=in_specs, out_specs=out_specs, check_vma=False)
```

profile of v0, /device:TPU:0, one launch (start us, length us, event | category | flops | bytes accessed | tf_op | source)
XLA Modules:
  0.0 1910.9 jit_solution(1182851010017177751)
XLA Ops:
  10.6 56.6 %all-gather.7.cloned.1.call-done = bf16[1152,1920]{1,0:T(8,128)(2,1)} async-done(((bf16[288,1920]{1,0:T(8,128)(2,1)}), bf16[1152,1920]{1,0:T(8,128)(2,1)}) %all-gather.7.cloned.1.call-update) | async-done | bytes 4423696 | tf_op jit(solution)/shard_map/all_gather | solution.py:205
  77.2 76.4 %all-reduce.6 = (s32[3072]{0:T(1024)S(1)}, s32[3072]{0:T(1024)S(1)}) all-reduce(s32[3072]{0:T(1024)S(1)} %dynamic-update-slice, s32[3072]{0:T(1024)S(1)} %dynamic-update-slice.1), channel_id=1, replica_groups=mesh['grp'=2,'ctx'=4,'wsh'=4] {'ctx','wsh'}, use_global_device_ids=true, to_apply=%add | all-reduce | flops 6144 | bytes 49152
  154.3 8.1 reshape.216
  168.4 31.3 %all-gather.9.cloned.1.call-done = bf16[3072,384]{1,0:T(8,128)(2,1)} async-done(((bf16[192,384]{1,0:T(8,128)(2,1)}), bf16[3072,384]{1,0:T(8,128)(2,1)}) %all-gather.9.cloned.1.call-update) | async-done | bytes 2359312 | tf_op jit(solution)/shard_map/all_gather | solution.py:226
  199.7 8.1 reshape.215
  215.0 24.5 %while.39 = (s32[]{:T(128)}, f32[6,3,192]{2,1,0:T(4,128)S(1)}, f32[6,3,192]{2,1,0:T(4,128)S(1)}, s32[3,1024]{1,0:T(4,128)S(1)}, s32[192]{0:T(256)S(1)}, /*index=...) while((s32[]{:T(128)}, f32[6,3,192]{2,1,0:T(4,128)S(1)}, ...), condition=%wide.region_4.5_spmd.clone, body=%wide.region_1.4_spmd.clone.sunk | while | flops 482101120 | bytes 30485644 | solution.py:111
  240.2 29.6 %while.40 = (s32[]{:T(128)}, f32[192,6,3,64]{0,3,2,1:T(8,128)}, bf16[3,1024,6,64]{1,3,2,0:T(8,128)(2,1)}, s32[3,1024]{1,0:T(4,128)S(1)}, s32[192]{0:T(256)S(1)},...) while((s32[]{:T(128)}, f32[192,6,3,64]{0,3,2,1:T(8,128)}, ...), condition=%wide.region_6.7_spmd.clone, body=%wide.region_5.6_spmd.clone.sunk | while | flops 924894208 | bytes 4674702 | solution.py:132
  242.0 7.8 fusion.126
  251.5 8.5 fusion.126
  261.7 8.2 fusion.126
  275.7 101.8 %all-gather.15.cloned.1.call-done = bf16[1152,6144]{1,0:T(8,128)(2,1)} async-done(((bf16[288,6144]{1,0:T(8,128)(2,1)}), bf16[1152,6144]{1,0:T(8,128)(2,1)}) %all-gather.15.cloned.1.call-update) | async-done | bytes 14155792 | tf_op jit(solution)/shard_map/all_gather | solution.py:207
  377.5 11.0 fusion.75
  388.5 67.5 %all-gather.17.cloned.1.call-done = bf16[3072,1152]{1,0:T(8,128)(2,1)} async-done(((bf16[768,1152]{1,0:T(8,128)(2,1)}), bf16[3072,1152]{1,0:T(8,128)(2,1)}) %all-gather.17.cloned.1.call-update) | async-done | bytes 7077904 | tf_op jit(solution)/shard_map/all_gather | solution.py:208
  455.9 8.8 multiply_convert_fusion.1
  464.7 11.3 multiply_reduce_fusion
  483.2 67.5 %while.41 = (s32[]{:T(128)}, f32[192,6,3,64]{0,3,2,1:T(8,128)}, f32[3,1024,6,64]{1,3,2,0:T(8,128)}, f32[3,1024,6,64]{1,3,2,0:T(8,128)}, bf16[3,1024,6,64]{1,3,2,...) while((s32[]{:T(128)}, f32[192,6,3,64]{0,3,2,1:T(8,128)}, ...), condition=%wide.region_10.11_spmd.clone, body=%wide.region_9.10_spmd.clone.sunk | while | flops 2308621312 | bytes 81001752 | solution.py:176
  493.4 7.3 fusion.138
  515.8 7.3 fusion.138
  538.1 7.4 fusion.138
  556.3 9.2 copy.76
  565.5 10.3 reshape.207
  575.9 9.2 copy.77
  585.1 10.4 reshape.209
  602.1 111.3 %reduce-scatter.19.cloned.1.call-done = f32[192,384]{1,0:T(8,128)} async-done(((f32[3072,384]{1,0:T(8,128)}), f32[192,384]{1,0:T(8,128)}) %reduce-scatter.19.cloned.1.call-update) | async-done | bytes 294928
  714.5 141.3 %reduce-scatter.21.cloned.1.call-done = f32[192,384]{1,0:T(8,128)} async-done(((f32[3072,384]{1,0:T(8,128)}), f32[192,384]{1,0:T(8,128)}) %reduce-scatter.21.cloned.1.call-update) | async-done | bytes 294928
  863.0 8.6 fusion.77
  872.8 12.6 fusion.51
  886.2 115.2 %reduce-scatter.25.cloned.1.call-done = f32[72,1152]{1,0:T(8,128)} async-done(((f32[1152,1152]{1,0:T(8,128)}), f32[72,1152]{1,0:T(8,128)}) %reduce-scatter.25.cloned.1.call-update) | async-done | bytes 331792
  1003.0 170.2 %reduce-scatter.23.cloned.1.call-done = f32[72,1920]{1,0:T(8,128)} async-done(((f32[1152,1920]{1,0:T(8,128)}), f32[72,1920]{1,0:T(8,128)}) %reduce-scatter.23.cloned.1.call-update) | async-done | bytes 552976
  1175.0 224.2 %reduce-scatter.17.cloned.1.call-done = f32[192,1152]{1,0:T(8,128)} async-done(((f32[3072,1152]{1,0:T(8,128)}), f32[192,1152]{1,0:T(8,128)}) %reduce-scatter.17.cloned.1.call-update) | async-done | bytes 884752 | tf_op jit(solution)/shard_map/reduce_scatter | solution.py:305
  1401.1 403.0 %reduce-scatter.15.cloned.1.call-done = f32[72,6144]{1,0:T(8,128)} async-done(((f32[1152,6144]{1,0:T(8,128)}), f32[72,6144]{1,0:T(8,128)}) %reduce-scatter.15.cloned.1.call-update) | async-done | bytes 1769488 | tf_op jit(solution)/shard_map/reduce_scatter | solution.py:304
  1816.6 74.8 %all-reduce.7 = (bf16[1152]{0:T(1024)(128)(2,1)S(1)}, bf16[1152]{0:T(1024)(128)(2,1)S(1)}) all-reduce(f32[1152]{0:T(1024)S(1)} %get-tuple-element.388, f32[1152]{0:T(1024)S(1)} %copy-done.29), channel_id=8, replica_groups=mesh['grp'=2,'ctx'=4,'wsh'=4] {'ctx','wsh'}, use_global_device_ids=true, to_apply=%region_23.24.clone | all-reduce | flops 2304 | bytes 13824
  (228 shorter events, 166.7 us)
Async XLA Ops:
  7.2 60.0 %all-gather.7.cloned.1.call-start = ((), (), s32[]{:S(2)}) async-start(), calls=%async_computation.6 | async-start | bytes 5529600 | tf_op jit(solution)/shard_map/all_gather | solution.py:205
  7.9 146.4 %all-gather.11.cloned.1.call-start = ((), (), s32[]{:S(2)}) async-start(), calls=%async_computation.8 | async-start | bytes 2506752 | tf_op jit(solution)/shard_map/all_gather | solution.py:225
  10.4 60.5 %copy-start.26 = (f32[192]{0:T(256)}, f32[192]{0:T(256)S(1)}, u32[]{:S(2)}) copy-start(f32[192]{0:T(256)S(1)} %get-tuple-element.488) | copy-start | bytes 2308
  10.6 143.4 %copy-start.14 = (f32[192,32]{0,1:T(8,128)}, f32[192,32]{0,1:T(8,128)S(1)}, u32[]{:S(2)}) copy-start(f32[192,32]{0,1:T(8,128)S(1)} %get-tuple-element.485) | copy-start | bytes 73732
  10.6 143.4 %copy-start.16 = (f32[192,32]{0,1:T(8,128)}, f32[192,32]{0,1:T(8,128)S(1)}, u32[]{:S(2)}) copy-start(f32[192,32]{0,1:T(8,128)S(1)} %get-tuple-element.486) | copy-start | bytes 73732
  72.0 127.7 %all-gather.9.cloned.1.call-start = ((), (), s32[]{:S(2)}) async-start(), calls=%async_computation.7 | async-start | bytes 2506752 | tf_op jit(solution)/shard_map/all_gather | solution.py:226
  72.8 199.3 %all-gather.13.cloned.1.call-start = ((), (), s32[]{:S(2)}) async-start(), calls=%async_computation.9 | async-start | bytes 3317760 | tf_op jit(solution)/shard_map/all_gather | solution.py:206
  73.3 304.2 %all-gather.15.cloned.1.call-start = ((), (), s32[]{:S(2)}) async-start(), calls=%async_computation.10 | async-start | bytes 17694720 | tf_op jit(solution)/shard_map/all_gather | solution.py:207
  73.9 382.0 %all-gather.17.cloned.1.call-start = ((), (), s32[]{:S(2)}) async-start(), calls=%async_computation.11 | async-start | bytes 8847360 | tf_op jit(solution)/shard_map/all_gather | solution.py:208
  74.5 638.9 %reduce-scatter.19.cloned.1.call-start = ((), (), s32[]{:S(2)}) async-start(), calls=%async_computation.14 | async-start | bytes 5013504
  240.2 31.8 %copy-start.7 = (bf16[192,1152]{1,0:T(8,128)(2,1)S(1)}, bf16[192,1152]{1,0:T(8,128)(2,1)}, u32[]{:S(2)}) copy-start(bf16[192,1152]{1,0:T(8,128)(2,1)} %param.16) | copy-start | bytes 1327108
  269.8 118.6 %copy-start.18 = (s32[3,1024]{1,0:T(4,128)}, s32[3,1024]{1,0:T(4,128)S(1)}, u32[]{:S(2)}) copy-start(s32[3,1024]{1,0:T(4,128)S(1)} %get-tuple-element.899) | copy-start | bytes 36868
  269.8 118.6 %copy-start.20 = (s32[192]{0:T(256)}, s32[192]{0:T(256)S(1)}, u32[]{:S(2)}) copy-start(s32[192]{0:T(256)S(1)} %get-tuple-element.902) | copy-start | bytes 2308
  269.8 107.7 %copy-start.21 = (f32[1152]{0:T(1024)S(1)}, f32[1152]{0:T(1024)}, u32[]{:S(2)}) copy-start(f32[1152]{0:T(1024)} %param.22) | copy-start | bytes 13828
  275.7 200.3 %copy-start.24 = (f32[192]{0:T(256)}, f32[192]{0:T(256)S(1)}, u32[]{:S(2)}) copy-start(f32[192]{0:T(256)S(1)} %get-tuple-element.490) | copy-start | bytes 2308
  377.5 78.4 %copy-start.11 = (bf16[192,1152]{1,0:T(8,128)(2,1)S(1)}, bf16[192,1152]{1,0:T(8,128)(2,1)}, u32[]{:S(2)}) copy-start(bf16[192,1152]{1,0:T(8,128)(2,1)} %param.25) | copy-start | bytes 1327108
  455.9 8.8 copy-start.3
  464.7 11.3 copy-start.13
  493.4 7.4 copy-start
  509.7 6.1 copy-start.28
  515.8 7.4 copy-start
  538.1 7.4 copy-start
  575.9 279.9 %reduce-scatter.21.cloned.1.call-start = ((), (), s32[]{:S(2)}) async-start(), calls=%async_computation.15 | async-start | bytes 5013504
  595.6 405.8 %reduce-scatter.25.cloned.1.call-start = ((), (), s32[]{:S(2)}) async-start(), calls=%async_computation.17 | async-start | bytes 5640192
  600.2 573.0 %reduce-scatter.23.cloned.1.call-start = ((), (), s32[]{:S(2)}) async-start(), calls=%async_computation.16 | async-start | bytes 9400320
  601.6 255.4 %copy-start.8 = (bf16[192,1152]{1,0:T(8,128)(2,1)S(1)}, bf16[192,1152]{1,0:T(8,128)(2,1)}, u32[]{:S(2)}) copy-start(bf16[192,1152]{1,0:T(8,128)(2,1)} %param.16) | copy-start | bytes 1327108
  601.6 255.4 %copy-start.23 = (f32[1152]{0:T(1024)S(1)}, f32[1152]{0:T(1024)}, u32[]{:S(2)}) copy-start(f32[1152]{0:T(1024)} %param.19) | copy-start | bytes 13828
  601.6 255.4 %copy-start.27 = (f32[192]{0:T(256)S(1)}, f32[192]{0:T(256)}, u32[]{:S(2)}) copy-start(f32[192]{0:T(256)} %copy-done.26) | copy-start | bytes 2308
  862.1 537.1 %reduce-scatter.17.cloned.1.call-start = ((), (), s32[]{:S(2)}) async-start(), calls=%async_computation.13 | async-start | bytes 15040512 | tf_op jit(solution)/shard_map/reduce_scatter | solution.py:305
  871.7 932.5 %reduce-scatter.15.cloned.1.call-start = ((), (), s32[]{:S(2)}) async-start(), calls=%async_computation.12 | async-start | bytes 30081024 | tf_op jit(solution)/shard_map/reduce_scatter | solution.py:304
  885.4 1010.8 %all-reduce.12.cloned.1.call-start = ((), (), s32[]{:S(2)}) async-start(), calls=%async_computation.18 | async-start | bytes 3538944 | tf_op jit(solution)/shard_map/psum | solution.py:310
  1812.5 82.5 %copy-start.30 = (f32[192]{0:T(256)S(1)}, f32[192]{0:T(256)}, u32[]{:S(2)}) copy-start(f32[192]{0:T(256)} %get-tuple-element.487) | copy-start | bytes 2308
  (19 other events, 47.1 us)
Sparse Core Ops, SparseCore 0:
  9.8 57.3 all-gather.6
  72.1 62.8 all-gather.10
  138.4 61.2 all-gather.8
  201.4 38.7 all-gather.12
  241.9 135.5 all-gather.14
  379.2 76.6 all-gather.16
  576.0 137.3 reduce-scatter.18
  719.4 136.3 reduce-scatter.20
  861.1 140.2 reduce-scatter.24
  1006.9 166.2 reduce-scatter.22
  1179.0 220.1 reduce-scatter.16
  1405.8 398.3 reduce-scatter.14
  1807.4 19.9 all-reduce.11
where the time goes:
time: 1920 us; the launch traced here: 1910 us
  waiting for transfers between devices  1420 us (74%)
  matrix products  173 us (9%)
  blocking collectives  154 us (8%)
  local copies, waits for them, and re-layouts  82.4 us (4%)
  other arithmetic  59.4 us (3%)
    unnamed x17, waiting for transfers between devices  540 us
    reduce_scatter x1, waiting for transfers between devices, local(): lax.psum_scatter(gate_up_grad, ('ctx', 'wsh'), scatter_dimension=0, tiled...  403 us
    reduce_scatter x1, waiting for transfers between devices, local(): lax.psum_scatter(down_grad, ('ctx', 'wsh'), scatter_dimension=0, tiled=True)  224 us
    unnamed x2, blocking collectives  151 us
    all_gather x1, waiting for transfers between devices, local(): lax.all_gather(gate_up, 'wsh', axis=0, tiled=True)  102 us
    all_gather x1, waiting for transfers between devices, local(): lax.all_gather(down_weight, 'wsh', axis=0, tiled=True)  67.5 us
    unnamed x73, local copies, waits for them, and re-layouts  62.7 us
    all_gather x1, waiting for transfers between devices, local(): lax.all_gather(query_key_value, 'wsh', axis=0, tiled=True)  56.6 us
  transfers between devices with their start and end apart: 13, of which 10 were waited for; matrix products, arithmetic and copies ran while one was open for 9% of the time, Pallas kernels for 0%

commit v1 on v0

--- a/solution.py
+++ b/solution.py
@@ -12,6 +12,18 @@
 QW = 1152
 KW = 384
 EPSILON = 1e-05
+
+
+def doubled_up(array, axis, dim):
+    ways, here = (lax.axis_size(axis), lax.axis_index(axis))
+    grown, reach = (array, 1)
+    while reach < ways:
+        theirs = lax.ppermute(grown, axis, [(d, d ^ reach) for d in range(ways)])
+        mine_first = jnp.concatenate([grown, theirs], axis=dim)
+        theirs_first = jnp.concatenate([theirs, grown], axis=dim)
+        grown = jnp.where(here & reach == 0, mine_first, theirs_first)
+        reach = 2 * reach
+    return grown
 
 
 def rope_angles(positions):
@@ -204,7 +216,7 @@
     full_qkv, full_out, full_gate_up, full_down = (
         lax.all_gather(query_key_value, "wsh", axis=0, tiled=True),
         lax.all_gather(attend_out, "wsh", axis=0, tiled=True),
-        lax.all_gather(gate_up, "wsh", axis=0, tiled=True),
+        doubled_up(gate_up, "wsh", 0),
         lax.all_gather(down_weight, "wsh", axis=0, tiled=True),
     )
     projected = jnp.dot(normed_one, full_qkv, preferred_element_type=jnp.float32)

time: 1920 us -> 2060 us (1.073)
  blocking collectives: 154 us -> 232 us
  matrix products: 173 us -> 216 us
    ppermute x0 -> x2, waiting for transfers between devices: none -> 143 us  [doubled_up(): theirs = lax.ppermute(grown, axis, [(d, d ^ reach) for d in range(ways)])]
    unnamed x2, blocking collectives: 151 us -> 229 us
    all_gather x1, waiting for transfers between devices: 67.5 us -> 0.01 us  [local(): lax.all_gather(down_weight, 'wsh', axis=0, tiled=True)]
    all_gather x1, waiting for transfers between devices: 102 us -> 52.1 us  [local(): lax.all_gather(gate_up, 'wsh', axis=0, tiled=True)]
    all_gather x1, waiting for transfers between devices: 31.3 us -> 0.02 us  [local(): lax.all_gather(value_local, ('ctx', 'wsh'), axis=0, tiled=True)]
    unnamed x73 -> x81, local copies, waits for them, and re-layouts: 62.7 us -> 66.3 us
  transfers between devices with their start and end apart: 13 -> 15, of which waited for: 10 -> 9; matrix products, arithmetic and copies ran while one was open for 9% -> 11% of each run, Pallas kernels for 0% -> 0%
where the time goes in v1:
time: 2060 us; the launch traced here: 2050 us
  waiting for transfers between devices  1420 us (69%)
  blocking collectives  232 us (11%)
  matrix products  216 us (10%)
  local copies, waits for them, and re-layouts  92.8 us (5%)
  other arithmetic  71.4 us (3%)
    unnamed x17, waiting for transfers between devices  542 us
    reduce_scatter x1, waiting for transfers between devices, local(): lax.psum_scatter(gate_up_grad, ('ctx', 'wsh'), scatter_dimension=0, tiled...  402 us
    unnamed x2, blocking collectives  229 us
    reduce_scatter x1, waiting for transfers between devices, local(): lax.psum_scatter(down_grad, ('ctx', 'wsh'), scatter_dimension=0, tiled=True)  224 us
    ppermute x2, waiting for transfers between devices, doubled_up(): theirs = lax.ppermute(grown, axis, [(d, d ^ reach) for d in range(ways)])  143 us
    unnamed x81, local copies, waits for them, and re-layouts  66.3 us
    all_gather x1, waiting for transfers between devices, local(): lax.all_gather(query_key_value, 'wsh', axis=0, tiled=True)  55.9 us
    all_gather x1, waiting for transfers between devices, local(): lax.all_gather(gate_up, 'wsh', axis=0, tiled=True)  52.1 us
  transfers between devices with their start and end apart: 15, of which 9 were waited for; matrix products, arithmetic and copies ran while one was open for 11% of the time, Pallas kernels for 0%

profile of v1, /device:TPU:0, one launch (start us, length us, event | category | flops | bytes accessed | tf_op | source)
XLA Modules:
  0.0 2049.8 jit_solution(8635507766335848485)
XLA Ops:
  11.3 55.9 %all-gather.7.cloned.1.call-done = bf16[1152,1920]{1,0:T(8,128)(2,1)} async-done(((bf16[288,1920]{1,0:T(8,128)(2,1)}), bf16[1152,1920]{1,0:T(8,128)(2,1)}) %all-gather.7.cloned.1.call-update) | async-done | bytes 4423696 | tf_op jit(solution)/shard_map/all_gather | solution.py:217
  89.0 154.4 %all-reduce.6 = (s32[3072]{0:T(1024)}, s32[3072]{0:T(1024)}) all-reduce(s32[3072]{0:T(1024)} %dynamic-update-slice, s32[3072]{0:T(1024)} %dynamic-update-slice.1), channel_id=1, replica_groups=mesh['grp'=2,'ctx'=4,'wsh'=4] {'ctx','wsh'}, use_global_device_ids=true, to_apply=%add | all-reduce | flops 6144 | bytes 49152
  254.5 8.2 reshape.216
  268.8 43.5 %while.39 = (s32[]{:T(128)}, f32[6,3,192]{2,1,0:T(4,128)S(1)}, f32[6,3,192]{2,1,0:T(4,128)S(1)}, s32[3,1024]{1,0:T(4,128)S(1)}, s32[192]{0:T(256)S(1)}, /*index=...) while((s32[]{:T(128)}, f32[6,3,192]{2,1,0:T(4,128)S(1)}, ...), condition=%wide.region_4.5_spmd.clone, body=%wide.region_1.4_spmd.clone.sunk | while | flops 482101120 | bytes 30485644 | solution.py:123
  275.5 8.0 select_reduce_fusion.2
  290.3 7.6 select_reduce_fusion.2
  312.4 8.2 reshape.215
  327.8 27.4 %while.40 = (s32[]{:T(128)}, f32[192,6,3,64]{0,3,2,1:T(8,128)}, bf16[3,1024,6,64]{1,3,2,0:T(8,128)(2,1)}, s32[3,1024]{1,0:T(4,128)S(1)}, s32[192]{0:T(256)S(1)},...) while((s32[]{:T(128)}, f32[192,6,3,64]{0,3,2,1:T(8,128)}, ...), condition=%wide.region_6.7_spmd.clone, body=%wide.region_5.6_spmd.clone.sunk | while | flops 924894208 | bytes 4674702 | solution.py:144
  329.0 7.8 fusion.132
  337.7 8.2 fusion.132
  346.9 8.2 fusion.132
  361.1 142.7 %collective-permute-done.1 = bf16[576,6144]{1,0:T(8,128)(2,1)} collective-permute-done((bf16[576,6144]{1,0:T(8,128)(2,1)}, bf16[576,6144]{1,0:T(8,128)(2,1)}, u32[]{:S(2)}, u32[]{:S(2)}) %collective-permute-start.1) | collective-permute-done | bytes 7077920 | tf_op jit(solution)/shard_map/ppermute | solution.py:21
  503.8 13.7 fusion.49
  517.5 9.1 multiply_convert_fusion.1
  526.5 52.1 %all-gather.17.cloned.1.call-done = bf16[1152,6144]{1,0:T(8,128)(2,1)} async-done(((bf16[288,6144]{1,0:T(8,128)(2,1)}), bf16[1152,6144]{1,0:T(8,128)(2,1)}) %all-gather.17.cloned.1.call-update) | async-done | bytes 14155792 | tf_op jit(solution)/shard_map/all_gather | solution.py:261
  578.6 12.3 multiply_reduce_fusion
  597.3 92.4 %while.41 = (s32[]{:T(128)}, f32[192,6,3,64]{0,3,2,1:T(8,128)}, f32[3,1024,6,64]{1,3,2,0:T(8,128)}, f32[3,1024,6,64]{1,3,2,0:T(8,128)}, bf16[3,1024,6,64]{1,3,2,...) while((s32[]{:T(128)}, f32[192,6,3,64]{0,3,2,1:T(8,128)}, ...), condition=%wide.region_10.11_spmd.clone, body=%wide.region_9.10_spmd.clone.sunk | while | flops 2308621312 | bytes 187093232 | solution.py:188
  600.1 9.6 fusion.144
  630.6 9.6 fusion.144
  661.4 9.6 fusion.144
  695.1 9.2 copy.76
  704.4 10.3 reshape.207
  714.8 9.2 copy.77
  724.0 10.4 reshape.209
  749.7 102.1 %reduce-scatter.19.cloned.1.call-done = f32[192,384]{1,0:T(8,128)} async-done(((f32[3072,384]{1,0:T(8,128)}), f32[192,384]{1,0:T(8,128)}) %reduce-scatter.19.cloned.1.call-update) | async-done | bytes 294928
  853.0 141.6 %reduce-scatter.21.cloned.1.call-done = f32[192,384]{1,0:T(8,128)} async-done(((f32[3072,384]{1,0:T(8,128)}), f32[192,384]{1,0:T(8,128)}) %reduce-scatter.21.cloned.1.call-update) | async-done | bytes 294928
  1002.1 12.5 fusion.58
  1015.2 124.5 %reduce-scatter.25.cloned.1.call-done = f32[72,1152]{1,0:T(8,128)} async-done(((f32[1152,1152]{1,0:T(8,128)}), f32[72,1152]{1,0:T(8,128)}) %reduce-scatter.25.cloned.1.call-update) | async-done | bytes 331792
  1141.4 224.2 %reduce-scatter.17.cloned.1.call-done = f32[192,1152]{1,0:T(8,128)} async-done(((f32[3072,1152]{1,0:T(8,128)}), f32[192,1152]{1,0:T(8,128)}) %reduce-scatter.17.cloned.1.call-update) | async-done | bytes 884752 | tf_op jit(solution)/shard_map/reduce_scatter | solution.py:317
  1367.5 171.6 %reduce-scatter.23.cloned.1.call-done = f32[72,1920]{1,0:T(8,128)} async-done(((f32[1152,1920]{1,0:T(8,128)}), f32[72,1920]{1,0:T(8,128)}) %reduce-scatter.23.cloned.1.call-update) | async-done | bytes 552976
  1540.9 402.2 %reduce-scatter.15.cloned.1.call-done = f32[72,6144]{1,0:T(8,128)} async-done(((f32[1152,6144]{1,0:T(8,128)}), f32[72,6144]{1,0:T(8,128)}) %reduce-scatter.15.cloned.1.call-update) | async-done | bytes 1769488 | tf_op jit(solution)/shard_map/reduce_scatter | solution.py:316
  1955.5 74.7 %all-reduce.7 = (bf16[1152]{0:T(1024)(128)(2,1)S(1)}, bf16[1152]{0:T(1024)(128)(2,1)S(1)}) all-reduce(f32[1152]{0:T(1024)S(1)} %get-tuple-element.388, f32[1152]{0:T(1024)S(1)} %copy-done.32), channel_id=8, replica_groups=mesh['grp'=2,'ctx'=4,'wsh'=4] {'ctx','wsh'}, use_global_device_ids=true, to_apply=%region_23.24.clone | all-reduce | flops 2304 | bytes 13824
  (235 shorter events, 215.5 us)
Async XLA Ops:
  7.2 60.0 %all-gather.7.cloned.1.call-start = ((), (), s32[]{:S(2)}) async-start(), calls=%async_computation.6 | async-start | bytes 5529600 | tf_op jit(solution)/shard_map/all_gather | solution.py:217
  7.9 246.6 %all-gather.11.cloned.1.call-start = ((), (), s32[]{:S(2)}) async-start(), calls=%async_computation.8 | async-start | bytes 2506752 | tf_op jit(solution)/shard_map/all_gather | solution.py:237
  10.4 56.8 %copy-start.28 = (f32[192]{0:T(256)}, f32[192]{0:T(256)S(1)}, u32[]{:S(2)}) copy-start(f32[192]{0:T(256)S(1)} %get-tuple-element.488) | copy-start | bytes 2308
  72.0 10.1 copy-start.3
  72.0 11.7 copy-start.34
  72.0 13.5 copy-start.21
  72.0 15.6 copy-start.23
  78.6 233.8 %all-gather.9.cloned.1.call-start = ((), (), s32[]{:S(2)}) async-start(), calls=%async_computation.7 | async-start | bytes 2506752 | tf_op jit(solution)/shard_map/all_gather | solution.py:238
  80.3 277.0 %all-gather.13.cloned.1.call-start = ((), (), s32[]{:S(2)}) async-start(), calls=%async_computation.9 | async-start | bytes 3317760 | tf_op jit(solution)/shard_map/all_gather | solution.py:218
  80.9 436.6 %all-gather.15.cloned.1.call-start = ((), (), s32[]{:S(2)}) async-start(), calls=%async_computation.10 | async-start | bytes 8847360 | tf_op jit(solution)/shard_map/all_gather | solution.py:220
  81.5 497.1 %all-gather.17.cloned.1.call-start = ((), (), s32[]{:S(2)}) async-start(), calls=%async_computation.11 | async-start | bytes 17694720 | tf_op jit(solution)/shard_map/all_gather | solution.py:261
  82.1 769.8 %reduce-scatter.19.cloned.1.call-start = ((), (), s32[]{:S(2)}) async-start(), calls=%async_computation.14 | async-start | bytes 5013504
  82.1 163.4 %collective-permute-start = (bf16[288,6144]{1,0:T(8,128)(2,1)S(1)}, bf16[288,6144]{1,0:T(8,128)(2,1)}, u32[]{:S(2)}, u32[]{:S(2)}) collective-permute-start(bf16[288,6144]{1,0:T(8,128)(2,1)S(1)} %copy-done.3), channel_id=1, source_target_pairs={{0,1},{1,0},{2,3},{3,2},{4,5},{5,4},{6,7},{7,6},{8,9},{9,8},{10,11... | collective-permute-start | bytes 10616840 | tf_op jit(solution)/shard_map/ppermute | solution.py:21
  252.9 250.9 %collective-permute-start.1 = (bf16[576,6144]{1,0:T(8,128)(2,1)}, bf16[576,6144]{1,0:T(8,128)(2,1)}, u32[]{:S(2)}, u32[]{:S(2)}) collective-permute-start(bf16[576,6144]{1,0:T(8,128)(2,1)} %maximum_select_fusion.2), channel_id=1, source_target_pairs={{0,2},{1,3},{2,0},{3,1},{4,6},{5,7},{6,4},{7,5},{8,10},{9,11},{10,... | collective-permute-start | bytes 21233672 | tf_op jit(solution)/shard_map/ppermute | solution.py:21
  327.8 29.6 %copy-start.6 = (bf16[192,1152]{1,0:T(8,128)(2,1)S(1)}, bf16[192,1152]{1,0:T(8,128)(2,1)}, u32[]{:S(2)}) copy-start(bf16[192,1152]{1,0:T(8,128)(2,1)} %param.16) | copy-start | bytes 1327108
  355.1 148.7 %copy-start.26 = (f32[1152]{0:T(1024)S(1)}, f32[1152]{0:T(1024)}, u32[]{:S(2)}) copy-start(f32[1152]{0:T(1024)} %param.22) | copy-start | bytes 13828
  361.1 229.9 %copy-start.30 = (f32[192]{0:T(256)}, f32[192]{0:T(256)S(1)}, u32[]{:S(2)}) copy-start(f32[192]{0:T(256)S(1)} %get-tuple-element.490) | copy-start | bytes 2308
  503.8 13.7 copy-start.14
  578.6 14.9 copy-start.8
  609.7 12.2 copy-start.1
  640.2 12.4 copy-start.1
  670.9 12.5 copy-start.1
  714.7 279.9 %reduce-scatter.21.cloned.1.call-start = ((), (), s32[]{:S(2)}) async-start(), calls=%async_computation.15 | async-start | bytes 5013504
  734.4 405.2 %reduce-scatter.25.cloned.1.call-start = ((), (), s32[]{:S(2)}) async-start(), calls=%async_computation.17 | async-start | bytes 5640192
  739.2 626.4 %reduce-scatter.17.cloned.1.call-start = ((), (), s32[]{:S(2)}) async-start(), calls=%async_computation.13 | async-start | bytes 15040512 | tf_op jit(solution)/shard_map/reduce_scatter | solution.py:317
  747.9 248.0 %copy-start.7 = (bf16[192,1152]{1,0:T(8,128)(2,1)S(1)}, bf16[192,1152]{1,0:T(8,128)(2,1)}, u32[]{:S(2)}) copy-start(bf16[192,1152]{1,0:T(8,128)(2,1)} %param.16) | copy-start | bytes 1327108
  747.9 247.9 %copy-start.25 = (f32[1152]{0:T(1024)S(1)}, f32[1152]{0:T(1024)}, u32[]{:S(2)}) copy-start(f32[1152]{0:T(1024)} %param.19) | copy-start | bytes 13828
  747.9 247.9 %copy-start.29 = (f32[192]{0:T(256)S(1)}, f32[192]{0:T(256)}, u32[]{:S(2)}) copy-start(f32[192]{0:T(256)} %copy-done.28) | copy-start | bytes 2308
  747.9 791.2 %reduce-scatter.23.cloned.1.call-start = ((), (), s32[]{:S(2)}) async-start(), calls=%async_computation.16 | async-start | bytes 9400320
  1000.9 942.1 %reduce-scatter.15.cloned.1.call-start = ((), (), s32[]{:S(2)}) async-start(), calls=%async_computation.12 | async-start | bytes 30081024 | tf_op jit(solution)/shard_map/reduce_scatter | solution.py:316
  1014.5 1020.5 %all-reduce.12.cloned.1.call-start = ((), (), s32[]{:S(2)}) async-start(), calls=%async_computation.18 | async-start | bytes 3538944 | tf_op jit(solution)/shard_map/psum | solution.py:322
  1951.4 82.5 %copy-start.33 = (f32[192]{0:T(256)S(1)}, f32[192]{0:T(256)}, u32[]{:S(2)}) copy-start(f32[192]{0:T(256)} %get-tuple-element.487) | copy-start | bytes 2308
  (22 other events, 86.8 us)
Sparse Core Ops, SparseCore 0:
  9.8 57.3 all-gather.6
  78.7 73.8 all-gather.10
  156.0 61.8 all-gather.8
  219.6 50.4 all-gather.12
  271.7 136.6 all-gather.14
  410.1 168.4 all-gather.16
  714.9 136.9 reduce-scatter.18
  857.8 136.7 reduce-scatter.20
  999.9 139.7 reduce-scatter.24
  1145.3 220.1 reduce-scatter.16
  1372.2 166.8 reduce-scatter.22
  1545.7 397.3 reduce-scatter.14
  1946.4 19.9 all-reduce.11
